TPU v7x, 32 devices: a whole 2x2x4 slice. The times are simulated.
32 devices in a mesh: freq: 2 (over y), bfly: 16 (over z, x, core).
Axes of the slice: x: 2, y: 2, z: 4, core: 2. Of those that a mesh axis runs over, the one named last changes fastest.
Arguments:
- coefficients: bfloat16 [32768, 512], P(('freq', 'bfly')), parts along dimension 0, may hold values from -6 to 6
- transfer: bfloat16 [5, 32768, 1024], P(None, ('freq', 'bfly')), parts along dimension 1, may hold values from -0.25 to 0.25
- ranks: int32 [6, 16], P(None, 'bfly'), may hold values from 256 to 1024, as said below
- owner_map: int32 [16], replicated, may hold values from 0 to 3, as said below
Outputs:
- target_field: bfloat16 [8192, 512], P(('freq', 'bfly')), parts along dimension 0
There are 2 independent parts, one for each index of `freq`. A program takes and returns all parts, laid end to end along the dimension named above; an argument that names none is the same for every part. Nothing has to cross between parts.
Inputs may be any that keep to these rules, and one draw needn't show every extreme that they name: Every row of ranks holds the value 1024 at least once. `owner_map`: within each aligned group of four blocks the four entries are a permutation of 0 to 3.
All inputs are finite; a program needn't handle non-finite values.
Results may differ from a plain program's by a relative error of at most 0.0095.
Values may be sent and summed in bfloat16 or wider, within the bound.
A program may use at most 64 MiB of HBM per device.

v0:
```python
import jax
import jax.numpy as jnp
from jax import lax
from jax.sharding import PartitionSpec as P

R = 1024
W = 512
LEVELS = 5


def from_partner(value, axis, apart):
    mask = 2**apart
    pairs = [(source, source ^ mask) for source in range(lax.axis_size(axis))]
    return lax.ppermute(value, axis, pairs)


def shards(coefficients, transfer, ranks, owner_map):
    half_rows = R // 2
    quarter = R // 4
    count = lax.axis_size("bfly")
    log_count = count.bit_length() - 1
    position = lax.axis_index("bfly")
    row_ids = jnp.arange(R, dtype=jnp.int32)
    current = jnp.where((row_ids < ranks[0, 0])[:, None], coefficients, jnp.zeros((), jnp.bfloat16))
    for level_idx in range(LEVELS):
        bit_pos = (log_count - 1 - level_idx) % log_count
        which_half = position >> bit_pos & 1
        paired_rows = current.reshape(half_rows, 2, W)
        own_half = lax.dynamic_index_in_dim(paired_rows, which_half, 1, keepdims=False)
        other_half = lax.dynamic_index_in_dim(paired_rows, 1 - which_half, 1, keepdims=False)
        received = from_partner(other_half, "bfly", bit_pos)
        matrix = transfer[level_idx]
        own_cols = lax.dynamic_slice_in_dim(matrix, which_half * half_rows, half_rows, 1)
        peer_cols = lax.dynamic_slice_in_dim(matrix, (1 - which_half) * half_rows, half_rows, 1)
        product = jnp.dot(own_cols, own_half, preferred_element_type=jnp.float32)
        product = product + jnp.dot(peer_cols, received, preferred_element_type=jnp.float32)
        keep_rows = (row_ids < ranks[level_idx + 1, 0])[:, None]
        current = jnp.where(keep_rows, product, jnp.float32(0.0)).astype(jnp.bfloat16)
    group_pos = position % 4
    group_idx = position // 4
    owners = lax.dynamic_slice_in_dim(owner_map, group_idx * 4, 4, 0)
    mine = owners[group_pos]
    quarters = current.reshape(4, quarter, W)

    def select_quarter(index):
        return lax.dynamic_index_in_dim(quarters, index, 0, keepdims=False)

    pair_mate = owners[group_pos ^ 1]
    far_first = owners[group_pos ^ 2]
    far_second = owners[group_pos ^ 3]
    outgoing = jnp.stack([select_quarter(far_first), select_quarter(far_second)])
    kept_pair = jnp.stack([select_quarter(mine), select_quarter(pair_mate)])
    incoming = from_partner(outgoing, "bfly", 1)
    partial_value = kept_pair.astype(jnp.float32) + incoming.astype(jnp.float32)
    mate_sum = from_partner(partial_value[1].astype(jnp.bfloat16), "bfly", 0).astype(jnp.float32)
    total = partial_value[0] + mate_sum
    return total.astype(jnp.bfloat16)


def solution(mesh):
    in_specs = (P(("freq", "bfly"), None), P(None, ("freq", "bfly"), None), P(None, "bfly"), P())
    out_specs = P(("freq", "bfly"), None)
    return jax.shard_map(shards, mesh=mesh, in_specs=in_specs, out_specs=out_specs, check_vma=False)
```

profile of v0, /device:TPU:0, one launch (start us, length us, event | category | flops | bytes accessed | tf_op | source)
XLA Modules:
  0.0 135.5 jit_solution(16034869629172434246)
XLA Ops:
  0.0 1.5 %fusion.42 = (s32[1,1]{0,1:T(1,128)}, s32[1,1]{0,1:T(1,128)}, s32[1,1]{0,1:T(1,128)}, s32[1,1]{0,1:T(1,128)}, s32[1,1]{0,1:T(1,128)}, /*index=5*/s32[1,1]{0,1:T(1,128)}) fusion(s32[6,1]{0,1:T(1,128)} %param.6), kind=kLoop, calls=%fused_computation.81 | loop fusion | bytes 48 | tf_op jit(solution)/shard_map/slice | solution.py:37
  2.1 1.4 %broadcast_select_fusion = bf16[1024,512]{1,0:T(8,128)(2,1)S(1)} fusion(bf16[1024,512]{1,0:T(8,128)(2,1)} %param.4, pred[1024]{0:T(1024)(128)(4,1)S(1)} %iota_compare_fusion), kind=kLoop, calls=%fused_computation.31 | loop fusion | flops 524288 | bytes 2098176 | tf_op jit(solution)/shard_map/jit(_where)/select_n | solution.py:24
  4.0 2.2 %constant_dynamic-slice_fusion.12 = (bf16[512,1,512]{2,1,0:T(2,128)(2,1)S(1)}, bf16[512,1,512]{2,1,0:T(2,128)(2,1)S(1)}) fusion(bf16[512,2,512]{2,1,0:T(2,128)(2,1)S(1)} %reshape.53, s32[]{:T(128)S(6)} %select_n.129, s32[]{:T(128)S(6)} %select_n.127), kind=kLoop, calls=%fused_computation.65 | loop fusion | bytes 2097160 | tf_op jit(solution)/shard_map/jit(dynamic_index_in_dim)/dynamic_slice | solution.py:30
  6.1 0.9 copy.52
  7.1 4.1 %collective-permute-start = (bf16[512,512]{1,0:T(8,128)(2,1)}, bf16[512,512]{1,0:T(8,128)(2,1)}, u32[]{:S(2)}, u32[]{:S(2)}) collective-permute-start(bf16[512,512]{1,0:T(8,128)(2,1)} %bitcast.83), channel_id=1, source_target_pairs={{0,8},{1,9},{2,10},{3,11},{4,12},{5,13},{6,14},{7,15},{8,0},{9,1},... | collective-permute-start | bytes 1572872 | tf_op jit(solution)/shard_map/ppermute | solution.py:14
  11.1 7.4 %fusion.40 = (bf16[1,1024,1024]{2,1,0:T(8,128)(2,1)}, bf16[1,1024,1024]{2,1,0:T(8,128)(2,1)}, bf16[1,1024,1024]{2,1,0:T(8,128)(2,1)}, bf16[1,1024,1024]{2,1,0:T(8,128)(2,1)S(1)}, bf16[1,1024,1024]{2,1,0:T(8,128)(2,1)}) fusion(bf16[5,1024,1024]{2,1,0:T(8,128)(2,1)} %param.5), kind=kLoop, calls=%fused_computation.79 | loop fusion | bytes 20971520 | tf_op jit(solution)/shard_map/slice | solution.py:32
  19.3 1.9 %fusion.5 = f32[1024,512]{1,0:T(8,128)S(1)} fusion(bf16[1,1024,1024]{2,1,0:T(8,128)(2,1)} %get-tuple-element.5, s32[]{:T(128)S(6)} %select_n.122, bf16[512,1,512]{2,1,0:T(2,128)(2,1)S(1)} %get-tuple-element.23), kind=kOutput, calls=%fused_computation.10 | convolution fusion | flops 536870912 | bytes 3670020 | tf_op jit(solution)/shard_map/dot_general | solution.py:35
  21.2 13.4 %collective-permute-done = bf16[512,512]{1,0:T(8,128)(2,1)} collective-permute-done((bf16[512,512]{1,0:T(8,128)(2,1)}, bf16[512,512]{1,0:T(8,128)(2,1)}, u32[]{:S(2)}, u32[]{:S(2)}) %collective-permute-start) | collective-permute-done | bytes 524320 | tf_op jit(solution)/shard_map/ppermute | solution.py:14
  34.6 2.7 %select_convert_fusion.4 = bf16[1024,512]{1,0:T(8,128)(2,1)} fusion(f32[1024,512]{1,0:T(8,128)S(1)} %fusion.5, bf16[512,512]{1,0:T(8,128)(2,1)} %collective-permute-done, bf16[1,1024,1024]{2,1,0:T(8,128)(2,1)S(1)} %copy-done.3, s32[]{:T(128)S(6)} %select_n.128, pred[1024]{0:T(1024)(128)(4,1)S(1)} %iota_compare_fusion.1), kind=kOutput, calls=%fused_computation.4 | convolution fusion | flops 538443776 | bytes 4719620 | tf_op jit(solution)/shard_map/dot_general | solution.py:36
  37.4 1.5 %reshape.54 = bf16[512,2,512]{2,1,0:T(2,128)(2,1)S(1)} reshape(bf16[1024,512]{1,0:T(8,128)(2,1)} %select_convert_fusion.4) | data formatting | bytes 2097152 | tf_op jit(solution)/shard_map/reshape | solution.py:28
  38.8 3.1 %constant_dynamic-slice_fusion.10 = (bf16[512,1,512]{2,1,0:T(2,128)(2,1)S(1)}, bf16[512,1,512]{2,1,0:T(2,128)(2,1)}) fusion(bf16[512,2,512]{2,1,0:T(2,128)(2,1)S(1)} %reshape.54, s32[]{:T(128)S(6)} %select_n.133, s32[]{:T(128)S(6)} %select_n.131), kind=kLoop, calls=%fused_computation.62 | loop fusion | bytes 2097160 | tf_op jit(solution)/shard_map/jit(dynamic_index_in_dim)/dynamic_slice | solution.py:30
  43.7 2.3 %fusion.7 = f32[1024,512]{1,0:T(8,128)S(1)} fusion(bf16[1,1024,1024]{2,1,0:T(8,128)(2,1)} %get-tuple-element.9, s32[]{:T(128)S(6)} %select_n.125, bf16[512,1,512]{2,1,0:T(2,128)(2,1)} %get-tuple-element.21), kind=kOutput, calls=%fused_computation.12 | convolution fusion | flops 536870912 | bytes 4194308 | tf_op jit(solution)/shard_map/dot_general | solution.py:35
  45.9 9.3 %collective-permute-done.1 = bf16[512,512]{1,0:T(8,128)(2,1)S(1)} collective-permute-done((bf16[512,512]{1,0:T(8,128)(2,1)S(1)}, bf16[512,512]{1,0:T(8,128)(2,1)S(1)}, u32[]{:S(2)}, u32[]{:S(2)}) %collective-permute-start.1) | collective-permute-done | bytes 524320 | tf_op jit(solution)/shard_map/ppermute | solution.py:14
  55.2 1.7 %select_convert_fusion.3 = bf16[1024,512]{1,0:T(8,128)(2,1)} fusion(f32[1024,512]{1,0:T(8,128)S(1)} %fusion.7, bf16[512,512]{1,0:T(8,128)(2,1)S(1)} %collective-permute-done.1, bf16[1,1024,1024]{2,1,0:T(8,128)(2,1)S(1)} %copy-done.2, s32[]{:T(128)S(6)} %select_n.132, pred[1024]{0:T(1024)(128)(4,1)S(1)} %iota_compare_fusion.2), kind=kOutput, calls=%fused_computation.3 | convolution fusion | flops 538443776 | bytes 4719620 | tf_op jit(solution)/shard_map/dot_general | solution.py:36
  57.0 1.6 %reshape.55 = bf16[512,2,512]{2,1,0:T(2,128)(2,1)S(1)} reshape(bf16[1024,512]{1,0:T(8,128)(2,1)} %select_convert_fusion.3) | data formatting | bytes 2097152 | tf_op jit(solution)/shard_map/reshape | solution.py:28
  58.6 3.1 %constant_dynamic-slice_fusion.8 = (bf16[512,1,512]{2,1,0:T(2,128)(2,1)S(1)}, bf16[512,1,512]{2,1,0:T(2,128)(2,1)}) fusion(bf16[512,2,512]{2,1,0:T(2,128)(2,1)S(1)} %reshape.55, s32[]{:T(128)S(6)} %select_n.137, s32[]{:T(128)S(6)} %select_n.135), kind=kLoop, calls=%fused_computation.59 | loop fusion | bytes 2097160 | tf_op jit(solution)/shard_map/jit(dynamic_index_in_dim)/dynamic_slice | solution.py:30
  61.9 1.4 collective-permute-start.2
  64.0 2.3 %fusion.9 = f32[1024,512]{1,0:T(8,128)S(1)} fusion(bf16[1,1024,1024]{2,1,0:T(8,128)(2,1)} %get-tuple-element.6, s32[]{:T(128)S(6)} %select_n.124, bf16[512,1,512]{2,1,0:T(2,128)(2,1)} %get-tuple-element.19), kind=kOutput, calls=%fused_computation.14 | convolution fusion | flops 536870912 | bytes 4194308 | tf_op jit(solution)/shard_map/dot_general | solution.py:35
  66.3 7.9 %collective-permute-done.2 = bf16[512,512]{1,0:T(8,128)(2,1)S(1)} collective-permute-done((bf16[512,512]{1,0:T(8,128)(2,1)S(1)}, bf16[512,512]{1,0:T(8,128)(2,1)S(1)}, u32[]{:S(2)}, u32[]{:S(2)}) %collective-permute-start.2) | collective-permute-done | bytes 524320 | tf_op jit(solution)/shard_map/ppermute | solution.py:14
  74.2 1.7 %select_convert_fusion.2 = bf16[1024,512]{1,0:T(8,128)(2,1)} fusion(f32[1024,512]{1,0:T(8,128)S(1)} %fusion.9, bf16[512,512]{1,0:T(8,128)(2,1)S(1)} %collective-permute-done.2, bf16[1,1024,1024]{2,1,0:T(8,128)(2,1)S(1)} %copy-done.1, s32[]{:T(128)S(6)} %select_n.136, pred[1024]{0:T(1024)(128)(4,1)S(1)} %iota_compare_fusion.3), kind=kOutput, calls=%fused_computation.2 | convolution fusion | flops 538443776 | bytes 4719620 | tf_op jit(solution)/shard_map/dot_general | solution.py:36
  75.9 1.5 %reshape.56 = bf16[512,2,512]{2,1,0:T(2,128)(2,1)S(1)} reshape(bf16[1024,512]{1,0:T(8,128)(2,1)} %select_convert_fusion.2) | data formatting | bytes 2097152 | tf_op jit(solution)/shard_map/reshape | solution.py:28
  77.4 3.1 %constant_dynamic-slice_fusion.6 = (bf16[512,1,512]{2,1,0:T(2,128)(2,1)S(1)}, bf16[512,1,512]{2,1,0:T(2,128)(2,1)}) fusion(bf16[512,2,512]{2,1,0:T(2,128)(2,1)S(1)} %reshape.56, s32[]{:T(128)S(6)} %select_n.141, s32[]{:T(128)S(6)} %select_n.139), kind=kLoop, calls=%fused_computation.56 | loop fusion | bytes 2097160 | tf_op jit(solution)/shard_map/jit(dynamic_index_in_dim)/dynamic_slice | solution.py:30
  81.5 2.3 %fusion.11 = f32[1024,512]{1,0:T(8,128)S(1)} fusion(bf16[1,1024,1024]{2,1,0:T(8,128)(2,1)} %get-tuple-element.7, s32[]{:T(128)S(6)} %select_n.123, bf16[512,1,512]{2,1,0:T(2,128)(2,1)} %get-tuple-element.17), kind=kOutput, calls=%fused_computation.16 | convolution fusion | flops 536870912 | bytes 4194308 | tf_op jit(solution)/shard_map/dot_general | solution.py:35
  83.8 1.7 %select_convert_fusion.1 = bf16[1024,512]{1,0:T(8,128)(2,1)} fusion(f32[1024,512]{1,0:T(8,128)S(1)} %fusion.11, bf16[512,512]{1,0:T(8,128)(2,1)S(1)} %collective-permute-done.3, bf16[1,1024,1024]{2,1,0:T(8,128)(2,1)S(1)} %copy-done, s32[]{:T(128)S(6)} %select_n.140, pred[1024]{0:T(1024)(128)(4,1)S(1)} %iota_compare_fusion.4), kind=kOutput, calls=%fused_computation.1 | convolution fusion | flops 538443776 | bytes 4719620 | tf_op jit(solution)/shard_map/dot_general | solution.py:36
  85.5 1.5 %reshape.57 = bf16[512,2,512]{2,1,0:T(2,128)(2,1)S(1)} reshape(bf16[1024,512]{1,0:T(8,128)(2,1)} %select_convert_fusion.1) | data formatting | bytes 2097152 | tf_op jit(solution)/shard_map/reshape | solution.py:28
  87.0 3.2 %constant_dynamic-slice_fusion.4 = (bf16[512,1,512]{2,1,0:T(2,128)(2,1)S(1)}, bf16[512,1,512]{2,1,0:T(2,128)(2,1)}) fusion(bf16[512,2,512]{2,1,0:T(2,128)(2,1)S(1)} %reshape.57, s32[]{:T(128)S(6)} %select_n.129, s32[]{:T(128)S(6)} %select_n.127), kind=kLoop, calls=%fused_computation.53 | loop fusion | bytes 2097160 | tf_op jit(solution)/shard_map/jit(dynamic_index_in_dim)/dynamic_slice | solution.py:30
  90.2 4.2 %collective-permute-start.4 = (bf16[512,512]{1,0:T(8,128)(2,1)S(1)}, bf16[512,512]{1,0:T(8,128)(2,1)S(1)}, u32[]{:S(2)}, u32[]{:S(2)}) collective-permute-start(bf16[512,512]{1,0:T(8,128)(2,1)S(1)} %bitcast.85), channel_id=1, source_target_pairs={{0,8},{1,9},{2,10},{3,11},{4,12},{5,13},{6,14},{7,15},{8,0},{9,1},... | collective-permute-start | bytes 1572872 | tf_op jit(solution)/shard_map/ppermute | solution.py:14
  103.3 1.9 %fusion.13 = f32[1024,512]{1,0:T(8,128)S(1)} fusion(bf16[1,1024,1024]{2,1,0:T(8,128)(2,1)S(1)} %get-tuple-element.8, s32[]{:T(128)S(6)} %select_n.122, bf16[512,1,512]{2,1,0:T(2,128)(2,1)} %get-tuple-element.15), kind=kOutput, calls=%fused_computation.18 | convolution fusion | flops 536870912 | bytes 3670020 | tf_op jit(solution)/shard_map/dot_general | solution.py:35
  105.2 13.1 %collective-permute-done.4 = bf16[512,512]{1,0:T(8,128)(2,1)S(1)} collective-permute-done((bf16[512,512]{1,0:T(8,128)(2,1)S(1)}, bf16[512,512]{1,0:T(8,128)(2,1)S(1)}, u32[]{:S(2)}, u32[]{:S(2)}) %collective-permute-start.4) | collective-permute-done | bytes 524320 | tf_op jit(solution)/shard_map/ppermute | solution.py:14
  119.2 1.5 %collective-permute-start.5 = (bf16[2,256,512]{2,1,0:T(8,128)(2,1)S(1)}, bf16[2,256,512]{2,1,0:T(8,128)(2,1)S(1)}, u32[]{:S(2)}, u32[]{:S(2)}) collective-permute-start(bf16[2,256,512]{2,1,0:T(8,128)(2,1)S(1)} %pad_maximum_fusion), channel_id=1, source_target_pairs={{0,2},{1,3},{2,0},{3,1},{4,6},{5,7},{6,4},{7,5},{8,10},{9,11},{10,... | collective-permute-start | bytes 1572872 | tf_op jit(solution)/shard_map/ppermute | solution.py:14
  120.7 12.2 %collective-permute-done.5 = bf16[2,256,512]{2,1,0:T(8,128)(2,1)S(1)} collective-permute-done((bf16[2,256,512]{2,1,0:T(8,128)(2,1)S(1)}, bf16[2,256,512]{2,1,0:T(8,128)(2,1)S(1)}, u32[]{:S(2)}, u32[]{:S(2)}) %collective-permute-start.5) | collective-permute-done | bytes 524320 | tf_op jit(solution)/shard_map/ppermute | solution.py:14
  133.2 1.5 %collective-permute-done.6 = bf16[256,512]{1,0:T(8,128)(2,1)S(1)} collective-permute-done((bf16[256,512]{1,0:T(8,128)(2,1)S(1)}, bf16[256,512]{1,0:T(8,128)(2,1)S(1)}, u32[]{:S(2)}, u32[]{:S(2)}) %collective-permute-start.6) | collective-permute-done | bytes 262176 | tf_op jit(solution)/shard_map/ppermute | solution.py:14
  (32 shorter events, 8.6 us)
Async XLA Ops:
  7.1 27.5 %collective-permute-start = (bf16[512,512]{1,0:T(8,128)(2,1)}, bf16[512,512]{1,0:T(8,128)(2,1)}, u32[]{:S(2)}, u32[]{:S(2)}) collective-permute-start(bf16[512,512]{1,0:T(8,128)(2,1)} %bitcast.83), channel_id=1, source_target_pairs={{0,8},{1,9},{2,10},{3,11},{4,12},{5,13},{6,14},{7,15},{8,0},{9,1},... | collective-permute-start | bytes 1572872 | tf_op jit(solution)/shard_map/ppermute | solution.py:14
  18.6 16.1 %copy-start.3 = (bf16[1,1024,1024]{2,1,0:T(8,128)(2,1)S(1)}, bf16[1,1024,1024]{2,1,0:T(8,128)(2,1)}, u32[]{:S(2)}) copy-start(bf16[1,1024,1024]{2,1,0:T(8,128)(2,1)} %get-tuple-element.5) | copy-start | bytes 6291460
  42.1 13.2 %collective-permute-start.1 = (bf16[512,512]{1,0:T(8,128)(2,1)S(1)}, bf16[512,512]{1,0:T(8,128)(2,1)S(1)}, u32[]{:S(2)}, u32[]{:S(2)}) collective-permute-start(bf16[512,512]{1,0:T(8,128)(2,1)S(1)} %bitcast.86), channel_id=1, source_target_pairs={{0,4},{1,5},{2,6},{3,7},{4,0},{5,1},{6,2},{7,3},{8,12},{9,13},{10,... | collective-permute-start | bytes 1572872 | tf_op jit(solution)/shard_map/ppermute | solution.py:14
  42.9 12.4 %copy-start.2 = (bf16[1,1024,1024]{2,1,0:T(8,128)(2,1)S(1)}, bf16[1,1024,1024]{2,1,0:T(8,128)(2,1)}, u32[]{:S(2)}) copy-start(bf16[1,1024,1024]{2,1,0:T(8,128)(2,1)} %get-tuple-element.9) | copy-start | bytes 6291460
  61.9 12.3 %collective-permute-start.2 = (bf16[512,512]{1,0:T(8,128)(2,1)S(1)}, bf16[512,512]{1,0:T(8,128)(2,1)S(1)}, u32[]{:S(2)}, u32[]{:S(2)}) collective-permute-start(bf16[512,512]{1,0:T(8,128)(2,1)S(1)} %bitcast.87), channel_id=1, source_target_pairs={{0,2},{1,3},{2,0},{3,1},{4,6},{5,7},{6,4},{7,5},{8,10},{9,11},{10,... | collective-permute-start | bytes 1572872 | tf_op jit(solution)/shard_map/ppermute | solution.py:14
  63.2 10.9 %copy-start.1 = (bf16[1,1024,1024]{2,1,0:T(8,128)(2,1)S(1)}, bf16[1,1024,1024]{2,1,0:T(8,128)(2,1)}, u32[]{:S(2)}) copy-start(bf16[1,1024,1024]{2,1,0:T(8,128)(2,1)} %get-tuple-element.6) | copy-start | bytes 6291460
  80.6 3.1 %collective-permute-start.3 = (bf16[512,512]{1,0:T(8,128)(2,1)S(1)}, bf16[512,512]{1,0:T(8,128)(2,1)S(1)}, u32[]{:S(2)}, u32[]{:S(2)}) collective-permute-start(bf16[512,512]{1,0:T(8,128)(2,1)S(1)} %bitcast.88), channel_id=1, source_target_pairs={{0,1},{1,0},{2,3},{3,2},{4,5},{5,4},{6,7},{7,6},{8,9},{9,8},{10,11... | collective-permute-start | bytes 1572872 | tf_op jit(solution)/shard_map/ppermute | solution.py:14
  80.7 3.0 %copy-start = (bf16[1,1024,1024]{2,1,0:T(8,128)(2,1)S(1)}, bf16[1,1024,1024]{2,1,0:T(8,128)(2,1)}, u32[]{:S(2)}) copy-start(bf16[1,1024,1024]{2,1,0:T(8,128)(2,1)} %get-tuple-element.7) | copy-start | bytes 6291460
  86.9 7.5 %copy-start.4 = (s32[16]{0:T(128)S(1)}, s32[16]{0:T(128)}, u32[]{:S(2)}) copy-start(s32[16]{0:T(128)} %param.7) | copy-start | bytes 196
  90.2 28.0 %collective-permute-start.4 = (bf16[512,512]{1,0:T(8,128)(2,1)S(1)}, bf16[512,512]{1,0:T(8,128)(2,1)S(1)}, u32[]{:S(2)}, u32[]{:S(2)}) collective-permute-start(bf16[512,512]{1,0:T(8,128)(2,1)S(1)} %bitcast.85), channel_id=1, source_target_pairs={{0,8},{1,9},{2,10},{3,11},{4,12},{5,13},{6,14},{7,15},{8,0},{9,1},... | collective-permute-start | bytes 1572872 | tf_op jit(solution)/shard_map/ppermute | solution.py:14
  119.2 13.8 %collective-permute-start.5 = (bf16[2,256,512]{2,1,0:T(8,128)(2,1)S(1)}, bf16[2,256,512]{2,1,0:T(8,128)(2,1)S(1)}, u32[]{:S(2)}, u32[]{:S(2)}) collective-permute-start(bf16[2,256,512]{2,1,0:T(8,128)(2,1)S(1)} %pad_maximum_fusion), channel_id=1, source_target_pairs={{0,2},{1,3},{2,0},{3,1},{4,6},{5,7},{6,4},{7,5},{8,10},{9,11},{10,... | collective-permute-start | bytes 1572872 | tf_op jit(solution)/shard_map/ppermute | solution.py:14
  133.1 1.6 %collective-permute-start.6 = (bf16[256,512]{1,0:T(8,128)(2,1)S(1)}, bf16[256,512]{1,0:T(8,128)(2,1)S(1)}, u32[]{:S(2)}, u32[]{:S(2)}) collective-permute-start(bf16[256,512]{1,0:T(8,128)(2,1)S(1)} %fusion.29), channel_id=1, source_target_pairs={{0,1},{1,0},{2,3},{3,2},{4,5},{5,4},{6,7},{7,6},{8,9},{9,8},{10,11... | collective-permute-start | bytes 786440 | tf_op jit(solution)/shard_map/ppermute | solution.py:14
where the time goes:
time: 136 us
  waiting for transfers between devices  57.4 us (42%)
  local copies, waits for them, and re-layouts  32.4 us (24%)
  matrix products  19.3 us (14%)
  starting transfers between devices  12.1 us (9%)
  between operations  7.7 us (6%)
  other arithmetic  6.6 us (5%)
    ppermute x7, waiting for transfers between devices, from_partner(): return lax.ppermute(value, axis, pairs)  57.4 us
    dynamic_slice x5, local copies, waits for them, and re-layouts, shards(): lax.dynamic_index_in_dim(paired_rows, 1 - which_half, 1, keepdims=False)  14.8 us
    ppermute x7, starting transfers between devices, from_partner(): return lax.ppermute(value, axis, pairs)  12.1 us
    dot_general x5, matrix products, shards(): product = jnp.dot(own_cols, own_half, preferred_element_type=jnp.float32)  10.7 us
    dot_general x5, matrix products, shards(): jnp.dot(peer_cols, received, preferred_element_type=jnp.float32)  8.62 us
    slice x1, local copies, waits for them, and re-layouts, shards(): matrix = transfer[level_idx]  7.41 us
    reshape x5, local copies, waits for them, and re-layouts, shards(): paired_rows = current.reshape(half_rows, 2, W)  6.48 us
    lt x5, other arithmetic, shards(): keep_rows = (row_ids < ranks[level_idx + 1, 0])[:, None]  3.64 us
  transfers between devices with their start and end apart: 7, of which 6 were waited for; matrix products, arithmetic and copies ran while one was open for 17% of the time, Pallas kernels for 0%

commit v1 on v0

v1 whole, which is shorter than its diff:
```python
import functools

import jax
import jax.numpy as jnp
from jax import lax
from jax.experimental import pallas as pl
from jax.experimental.pallas import tpu as pltpu
from jax.sharding import PartitionSpec as P

LANES = 128
GROUP = 4
F32 = jnp.float32
BF16 = jnp.bfloat16


def schedule(levels, chunks):
    order = []
    arrive = [7.2, 12.5, 16.5, 18.5, 29.0]
    for c in range(chunks):
        for level in range(levels):
            base = arrive[level] if level < len(arrive) else arrive[-1] + level
            order.append((base + 5.6 * c, "level", level, c))
        order.append((arrive[-1] + 4.4 + 5.6 * c, "final", levels, c))
        order.append((0.0 if c < 2 else 7.3 + 5.6 * (c - 2), "first", -1, c))
    return sorted(order)


def kernel(levels, count, ranks, owners, coef, transfer, out, m, xin, ybuf, acc, zown, zsend, zrecv, yfin, fsend, frecv,
           m_sem, x_sem, z_ssem, z_rsem, f_ssem, f_rsem):
    rows, width = coef.shape
    half, quarter, chunks = rows // 2, rows // GROUP, width // LANES
    log_count = count.bit_length() - 1
    pos = lax.axis_index("bfly")
    bits = [(log_count - 1 - level) % log_count for level in range(levels)]

    def bit_of(b):
        return (pos // 2**b) % 2

    def partner(mask):
        where = pos
        for b in range(log_count):
            if mask >> b & 1:
                where = where + (1 - 2 * bit_of(b)) * 2**b
        return where

    x_copies = [pltpu.make_async_copy(coef.at[:, pl.ds(c * LANES, LANES)], xin.at[c], x_sem.at[c]) for c in range(chunks)]
    for copy in x_copies:
        copy.start()
    m_copies = []
    for level in range(levels):
        s = bit_of(bits[level])
        for side, start in ((0, s), (1, 1 - s)):
            cols = pl.ds(pl.multiple_of(start * half, half), half)
            copy = pltpu.make_async_copy(transfer.at[level, :, cols], m.at[level, side], m_sem.at[level, side])
            copy.start()
            m_copies.append(copy)
    masks = sorted({2**b for b in bits} | set(range(1, GROUP)))
    barrier = pltpu.get_barrier_semaphore()
    for mask in masks:
        pl.semaphore_signal(barrier, inc=1, device_id={"bfly": partner(mask)}, device_id_type=pl.DeviceIdType.MESH)
    pl.semaphore_wait(barrier, len(masks))

    loaded = set()

    def matrix(level, side):
        if (level, side) not in loaded:
            loaded.add((level, side))
            m_copies[2 * level + side].wait()
        return m[level, side]

    row_ids = lax.broadcasted_iota(jnp.int32, (rows, LANES), 0)
    z_copies, f_copies = {}, {}

    def spread(level, c, value):
        s = bit_of(bits[level])
        ybuf[...] = jnp.where(row_ids < ranks[level, 0], value, F32(0.0))
        even = ybuf[pl.ds(0, half, stride=2), :].astype(BF16)
        odd = ybuf[pl.ds(1, half, stride=2), :].astype(BF16)
        low = jnp.broadcast_to(s, even.shape) == 0
        zsend[level, c] = jnp.where(low, odd, even)
        copy = pltpu.make_async_remote_copy(
            zsend.at[level, c], zrecv.at[level, c], z_ssem.at[level, c], z_rsem.at[level, c],
            device_id={"bfly": partner(2 ** bits[level])}, device_id_type=pl.DeviceIdType.MESH)
        copy.start()
        z_copies[level, c] = copy
        zown[c] = jnp.where(low, even, odd)
        acc[c] = jnp.dot(matrix(level, 0), zown[c], preferred_element_type=F32)

    def owned(mask):
        return owners[(pos // GROUP) * GROUP + partner(mask) % GROUP]

    def picked(c, mask):
        which = jnp.full((quarter, LANES), owned(mask), jnp.int32)
        value = yfin[c, :quarter, :]
        for q in range(1, GROUP):
            value = jnp.where(which == q, yfin[c, q * quarter:(q + 1) * quarter, :], value)
        return value

    for _, kind, level, c in schedule(levels, chunks):
        if kind == "first":
            x_copies[c].wait()
            spread(0, c, xin[c].astype(F32))
        elif kind == "level":
            z_copies[level, c].wait_recv()
            product = acc[c] + jnp.dot(matrix(level, 1), zrecv[level, c], preferred_element_type=F32)
            if level + 1 < levels:
                spread(level + 1, c, product)
            else:
                kept = jnp.where(row_ids < ranks[levels, 0], product, F32(0.0))
                yfin[c] = kept.astype(BF16).astype(F32)
                for mask in range(GROUP - 1, 0, -1):
                    fsend[c, mask - 1] = picked(c, mask).astype(BF16)
                    copy = pltpu.make_async_remote_copy(
                        fsend.at[c, mask - 1], frecv.at[c, mask - 1], f_ssem.at[c, mask - 1], f_rsem.at[c, mask - 1],
                        device_id={"bfly": partner(mask)}, device_id_type=pl.DeviceIdType.MESH)
                    copy.start()
                    f_copies[c, mask] = copy
        else:
            total = picked(c, 0)
            for mask in range(1, GROUP):
                f_copies[c, mask].wait_recv()
                total = total + frecv[c, mask - 1].astype(F32)
            out[:, c * LANES:(c + 1) * LANES] = total.astype(BF16)
    for copy in list(z_copies.values()) + list(f_copies.values()):
        copy.wait_send()


def shards(coefficients, transfer, ranks, owner_map):
    rows, width = coefficients.shape
    levels = transfer.shape[0]
    count = lax.axis_size("bfly")
    half, quarter, chunks = rows // 2, rows // GROUP, width // LANES
    dma = pltpu.SemaphoreType.DMA
    return pl.pallas_call(
        functools.partial(kernel, levels, count),
        out_shape=jax.ShapeDtypeStruct((quarter, width), BF16),
        in_specs=[pl.BlockSpec(memory_space=pltpu.SMEM)] * 2 + [pl.BlockSpec(memory_space=pl.ANY)] * 2,
        out_specs=pl.BlockSpec(memory_space=pltpu.VMEM),
        scratch_shapes=[
            pltpu.VMEM((levels, 2, rows, half), BF16),
            pltpu.VMEM((chunks, rows, LANES), BF16),
            pltpu.VMEM((rows, LANES), F32),
            pltpu.VMEM((chunks, rows, LANES), F32),
            pltpu.VMEM((chunks, half, LANES), BF16),
            pltpu.VMEM((levels, chunks, half, LANES), BF16),
            pltpu.VMEM((levels, chunks, half, LANES), BF16),
            pltpu.VMEM((chunks, rows, LANES), F32),
            pltpu.VMEM((chunks, GROUP - 1, quarter, LANES), BF16),
            pltpu.VMEM((chunks, GROUP - 1, quarter, LANES), BF16),
            dma((levels, 2)),
            dma((chunks,)),
            dma((levels, chunks)),
            dma((levels, chunks)),
            dma((chunks, GROUP - 1)),
            dma((chunks, GROUP - 1)),
        ],
        compiler_params=pltpu.CompilerParams(collective_id=0, has_side_effects=True, vmem_limit_bytes=56 * 2**20),
    )(ranks, owner_map, coefficients, transfer)


def solution(mesh):
    in_specs = (P(("freq", "bfly"), None), P(None, ("freq", "bfly"), None), P(None, "bfly"), P())
    out_specs = P(("freq", "bfly"), None)
    return jax.shard_map(shards, mesh=mesh, in_specs=in_specs, out_specs=out_specs, check_vma=False)
```

time: 136 us -> 73.8 us (0.54)
  Pallas kernels: 0 us -> 70.6 us
  waiting for transfers between devices: 57.4 us -> 0 us
  local copies, waits for them, and re-layouts: 32.4 us -> 3 us
  matrix products: 19.3 us -> 0 us
  starting transfers between devices: 12.1 us -> 0 us
  between operations: 7.7 us -> 0.01 us
  other arithmetic: 6.6 us -> 0 us
    pallas_call x0 -> x1, Pallas kernels: none -> 70.6 us  [shards(): pl.pallas_call(functools.partial(kernel, levels, count), out_shape=jax.Sh...]
    ppermute x7 -> x0, waiting for transfers between devices: 57.4 us -> none  [from_partner(): return lax.ppermute(value, axis, pairs)]
    dot_general x10 -> x0, matrix products: 19.3 us -> none  [the longest x5 10.7 us: shards(): product = jnp.dot(own_cols, own_half, preferred_element_type=jnp.float32)]
    dynamic_slice x7 -> x0, local copies, waits for them, and re-layouts: 15.5 us -> none  [the longest x5 14.8 us: shards(): lax.dynamic_index_in_dim(paired_rows, 1 - which_half, 1, keepdims=False)]
    ppermute x7 -> x0, starting transfers between devices: 12.1 us -> none  [from_partner(): return lax.ppermute(value, axis, pairs)]
    slice x2 -> x0, local copies, waits for them, and re-layouts: 8.91 us -> none  [the longest x1 7.41 us: shards(): matrix = transfer[level_idx]]
    reshape x5 -> x0, local copies, waits for them, and re-layouts: 6.48 us -> none  [shards(): paired_rows = current.reshape(half_rows, 2, W)]
    lt x6 -> x0, other arithmetic: 4.2 us -> none  [the longest x5 3.64 us: shards(): keep_rows = (row_ids < ranks[level_idx + 1, 0])[:, None]]
  transfers between devices with their start and end apart: 7 -> 0, of which waited for: 6 -> 0; matrix products, arithmetic and copies ran while one was open for 17% -> 0% of each run, Pallas kernels for 0% -> 0%
where the time goes in v1:
time: 73.8 us; the launch traced here: 73.7 us
  Pallas kernels  70.6 us (96%)
  local copies, waits for them, and re-layouts  3 us (4%)
    pallas_call x1, Pallas kernels, shards(): pl.pallas_call(functools.partial(kernel, levels, count), out_shape=jax.Sh...  70.6 us
    unnamed x2, local copies, waits for them, and re-layouts  3 us

profile of v1, /device:TPU:0, one launch (start us, length us, event | category | flops | bytes accessed | tf_op | source)
XLA Modules:
  0.0 73.7 jit_solution(5930422996206779707)
XLA Ops:
  0.0 1.3 %copy.5.ranks = s32[6,1]{1,0:T(8,128)} copy(s32[6,1]{0,1:T(1,128)} %param.6) | data formatting | bytes 48 | tf_op args[2]
  1.3 70.6 %shard_map.46 = bf16[256,512]{1,0:T(8,128)(2,1)} custom-call(s32[6,1]{1,0:T(8,128)} %copy.5.ranks, s32[16]{0:T(128)} %owners.1, bf16[1024,512]{1,0:T(8,128)(2,1)} %coef.1, bf16[5,1024,1024]{2,1,0:T(8,128)(2,1)} %transfer.1), custom_call_target="tpu_custom_call" | custom-call | tf_op jit(solution)/shard_map/pallas_call | solution.py:134
  72.0 1.7 %copy.7 = bf16[256,512]{1,0:T(8,128)(2,1)} copy(bf16[256,512]{1,0:T(8,128)(2,1)} %shard_map.46) | data formatting | bytes 524288

commit v2 on v1

--- a/solution.py
+++ b/solution.py
@@ -9,19 +9,21 @@
 
 LANES = 128
 GROUP = 4
+PIECES = 1
 F32 = jnp.float32
 BF16 = jnp.bfloat16
 
 
 def schedule(levels, chunks):
     order = []
-    arrive = [7.2, 12.5, 16.5, 18.5, 29.0]
+    arrive = [7.2, 12.9, 18.5, 21.5, 29.0]
+    firsts = [0, 0, 7.3, 12.95]
     for c in range(chunks):
         for level in range(levels):
-            base = arrive[level] if level < len(arrive) else arrive[-1] + level
-            order.append((base + 5.6 * c, "level", level, c))
+            at = arrive[level] if level < len(arrive) else arrive[-1] + level
+            order.append((at + 5.6 * c, "level", level, c))
         order.append((arrive[-1] + 4.4 + 5.6 * c, "final", levels, c))
-        order.append((0.0 if c < 2 else 7.3 + 5.6 * (c - 2), "first", -1, c))
+        order.append((firsts[c], "first", -1, c))
     return sorted(order)
 
 
@@ -58,7 +60,6 @@
     barrier = pltpu.get_barrier_semaphore()
     for mask in masks:
         pl.semaphore_signal(barrier, inc=1, device_id={"bfly": partner(mask)}, device_id_type=pl.DeviceIdType.MESH)
-    pl.semaphore_wait(barrier, len(masks))
 
     loaded = set()
 
@@ -68,22 +69,31 @@
             m_copies[2 * level + side].wait()
         return m[level, side]
 
-    row_ids = lax.broadcasted_iota(jnp.int32, (rows, LANES), 0)
+    part = rows // PIECES
+    row_ids = lax.broadcasted_iota(jnp.int32, (part, LANES), 0)
     z_copies, f_copies = {}, {}
 
-    def spread(level, c, value):
+    def masked(level, piece, value):
+        return jnp.where(row_ids < ranks[level] - piece * part, value, F32(0.0))
+
+    def spread(level, c, rows_of_x):
         s = bit_of(bits[level])
-        ybuf[...] = jnp.where(row_ids < ranks[level, 0], value, F32(0.0))
-        even = ybuf[pl.ds(0, half, stride=2), :].astype(BF16)
-        odd = ybuf[pl.ds(1, half, stride=2), :].astype(BF16)
-        low = jnp.broadcast_to(s, even.shape) == 0
-        zsend[level, c] = jnp.where(low, odd, even)
-        copy = pltpu.make_async_remote_copy(
-            zsend.at[level, c], zrecv.at[level, c], z_ssem.at[level, c], z_rsem.at[level, c],
-            device_id={"bfly": partner(2 ** bits[level])}, device_id_type=pl.DeviceIdType.MESH)
-        copy.start()
-        z_copies[level, c] = copy
-        zown[c] = jnp.where(low, even, odd)
+        depth = part // 2
+        for p in range(PIECES):
+            at = pl.ds(p * depth, depth)
+            ybuf[p] = masked(level, p, rows_of_x(pl.ds(p * part, part)))
+            even = ybuf[p, pl.ds(0, depth, stride=2), :].astype(BF16)
+            odd = ybuf[p, pl.ds(1, depth, stride=2), :].astype(BF16)
+            low = jnp.broadcast_to(s, even.shape) == 0
+            zsend[level, c, at] = jnp.where(low, odd, even)
+            if not z_copies:
+                pl.semaphore_wait(barrier, len(masks))
+            copy = pltpu.make_async_remote_copy(
+                zsend.at[level, c, at], zrecv.at[level, c, at], z_ssem.at[level, c, p], z_rsem.at[level, c, p],
+                device_id={"bfly": partner(2 ** bits[level])}, device_id_type=pl.DeviceIdType.MESH)
+            copy.start()
+            z_copies[level, c, p] = copy
+            zown[c, at] = jnp.where(low, even, odd)
         acc[c] = jnp.dot(matrix(level, 0), zown[c], preferred_element_type=F32)
 
     def owned(mask):
@@ -99,15 +109,21 @@
     for _, kind, level, c in schedule(levels, chunks):
         if kind == "first":
             x_copies[c].wait()
-            spread(0, c, xin[c].astype(F32))
+            spread(0, c, lambda at: xin[c, at].astype(F32))
         elif kind == "level":
-            z_copies[level, c].wait_recv()
-            product = acc[c] + jnp.dot(matrix(level, 1), zrecv[level, c], preferred_element_type=F32)
+            for p in range(PIECES):
+                z_copies[level, c, p].wait_recv()
+            matrix(level, 1)
+
+            def product(at):
+                return acc[c, at] + jnp.dot(m[level, 1, at], zrecv[level, c], preferred_element_type=F32)
+
             if level + 1 < levels:
                 spread(level + 1, c, product)
             else:
-                kept = jnp.where(row_ids < ranks[levels, 0], product, F32(0.0))
-                yfin[c] = kept.astype(BF16).astype(F32)
+                for p in range(PIECES):
+                    at = pl.ds(p * part, part)
+                    yfin[c, at] = masked(levels, p, product(at)).astype(BF16).astype(F32)
                 for mask in range(GROUP - 1, 0, -1):
                     fsend[c, mask - 1] = picked(c, mask).astype(BF16)
                     copy = pltpu.make_async_remote_copy(
@@ -139,7 +155,7 @@
         scratch_shapes=[
             pltpu.VMEM((levels, 2, rows, half), BF16),
             pltpu.VMEM((chunks, rows, LANES), BF16),
-            pltpu.VMEM((rows, LANES), F32),
+            pltpu.VMEM((PIECES, rows // PIECES, LANES), F32),
             pltpu.VMEM((chunks, rows, LANES), F32),
             pltpu.VMEM((chunks, half, LANES), BF16),
             pltpu.VMEM((levels, chunks, half, LANES), BF16),
@@ -149,13 +165,13 @@
             pltpu.VMEM((chunks, GROUP - 1, quarter, LANES), BF16),
             dma((levels, 2)),
             dma((chunks,)),
-            dma((levels, chunks)),
-            dma((levels, chunks)),
+            dma((levels, chunks, PIECES)),
+            dma((levels, chunks, PIECES)),
             dma((chunks, GROUP - 1)),
             dma((chunks, GROUP - 1)),
         ],
         compiler_params=pltpu.CompilerParams(collective_id=0, has_side_effects=True, vmem_limit_bytes=56 * 2**20),
-    )(ranks, owner_map, coefficients, transfer)
+    )(ranks.reshape(-1), owner_map, coefficients, transfer)
 
 
 def solution(mesh):

time: 73.8 us -> 68.5 us (0.928)
  Pallas kernels: 70.6 us -> 66.7 us
  local copies, waits for them, and re-layouts: 3 us -> 1.67 us
    pallas_call x1, Pallas kernels: 70.6 us -> 66.7 us  [shards(): pl.pallas_call(functools.partial(kernel, levels, count), out_shape=jax.Sh...]
    unnamed x2 -> x1, local copies, waits for them, and re-layouts: 3 us -> 1.67 us
where the time goes in v2:
time: 68.5 us; the launch traced here: 68.4 us
  Pallas kernels  66.7 us (97%)
  local copies, waits for them, and re-layouts  1.67 us (2%)
    pallas_call x1, Pallas kernels, shards(): pl.pallas_call(functools.partial(kernel, levels, count), out_shape=jax.Sh...  66.7 us
    unnamed x1, local copies, waits for them, and re-layouts  1.67 us

profile of v2, /device:TPU:0, one launch (start us, length us, event | category | flops | bytes accessed | tf_op | source)
XLA Modules:
  0.0 68.4 jit_solution(6057633699993045853)
XLA Ops:
  0.0 66.7 %shard_map.46 = bf16[256,512]{1,0:T(8,128)(2,1)} custom-call(s32[6]{0:T(128)} %bitcast.1, s32[16]{0:T(128)} %owners.1, bf16[1024,512]{1,0:T(8,128)(2,1)} %coef.1, bf16[5,1024,1024]{2,1,0:T(8,128)(2,1)} %transfer.1), custom_call_target="tpu_custom_call" | custom-call | tf_op jit(solution)/shard_map/pallas_call | solution.py:150
  66.7 1.7 %copy.6 = bf16[256,512]{1,0:T(8,128)(2,1)} copy(bf16[256,512]{1,0:T(8,128)(2,1)} %shard_map.46) | data formatting | bytes 524288

commit v3 on v2

--- a/solution.py
+++ b/solution.py
@@ -16,13 +16,13 @@
 
 def schedule(levels, chunks):
     order = []
-    arrive = [7.2, 12.9, 18.5, 21.5, 29.0]
+    arrive = [7.2, 12.9, 18.5, 21.5, 33.5]
     firsts = [0, 0, 7.3, 12.95]
     for c in range(chunks):
         for level in range(levels):
             at = arrive[level] if level < len(arrive) else arrive[-1] + level
             order.append((at + 5.6 * c, "level", level, c))
-        order.append((arrive[-1] + 4.4 + 5.6 * c, "final", levels, c))
+        order.append((arrive[-1] + 10.0 + 5.6 * c, "final", levels, c))
         order.append((firsts[c], "first", -1, c))
     return sorted(order)
 
@@ -45,6 +45,10 @@
                 where = where + (1 - 2 * bit_of(b)) * 2**b
         return where
 
+    masks = sorted({2**b for b in bits} | set(range(1, GROUP)))
+    barrier = pltpu.get_barrier_semaphore()
+    for mask in masks:
+        pl.semaphore_signal(barrier, inc=1, device_id={"bfly": partner(mask)}, device_id_type=pl.DeviceIdType.MESH)
     x_copies = [pltpu.make_async_copy(coef.at[:, pl.ds(c * LANES, LANES)], xin.at[c], x_sem.at[c]) for c in range(chunks)]
     for copy in x_copies:
         copy.start()
@@ -54,13 +58,7 @@
         for side, start in ((0, s), (1, 1 - s)):
             cols = pl.ds(pl.multiple_of(start * half, half), half)
             copy = pltpu.make_async_copy(transfer.at[level, :, cols], m.at[level, side], m_sem.at[level, side])
-            copy.start()
             m_copies.append(copy)
-    masks = sorted({2**b for b in bits} | set(range(1, GROUP)))
-    barrier = pltpu.get_barrier_semaphore()
-    for mask in masks:
-        pl.semaphore_signal(barrier, inc=1, device_id={"bfly": partner(mask)}, device_id_type=pl.DeviceIdType.MESH)
-
     loaded = set()
 
     def matrix(level, side):
@@ -93,6 +91,9 @@
                 device_id={"bfly": partner(2 ** bits[level])}, device_id_type=pl.DeviceIdType.MESH)
             copy.start()
             z_copies[level, c, p] = copy
+            if len(z_copies) == 1:
+                for load in m_copies:
+                    load.start()
             zown[c, at] = jnp.where(low, even, odd)
         acc[c] = jnp.dot(matrix(level, 0), zown[c], preferred_element_type=F32)
 

time: 68.5 us -> 68.2 us (level)
  no operation moved by 1% of the time
where the time goes in v3:
time: 68.2 us; the launch traced here: 68 us
  Pallas kernels  66.3 us (97%)
  local copies, waits for them, and re-layouts  1.67 us (2%)
    pallas_call x1, Pallas kernels, shards(): pl.pallas_call(functools.partial(kernel, levels, count), out_shape=jax.Sh...  66.3 us
    unnamed x1, local copies, waits for them, and re-layouts  1.67 us

profile of v3, /device:TPU:0, one launch (start us, length us, event | category | flops | bytes accessed | tf_op | source)
XLA Modules:
  0.0 68.0 jit_solution(14813242457932697758)
XLA Ops:
  0.0 66.3 %shard_map.46 = bf16[256,512]{1,0:T(8,128)(2,1)} custom-call(s32[6]{0:T(128)} %bitcast.1, s32[16]{0:T(128)} %owners.1, bf16[1024,512]{1,0:T(8,128)(2,1)} %coef.1, bf16[5,1024,1024]{2,1,0:T(8,128)(2,1)} %transfer.1), custom_call_target="tpu_custom_call" | custom-call | tf_op jit(solution)/shard_map/pallas_call | solution.py:151
  66.3 1.7 %copy.6 = bf16[256,512]{1,0:T(8,128)(2,1)} copy(bf16[256,512]{1,0:T(8,128)(2,1)} %shard_map.46) | data formatting | bytes 524288

commit v4 on v3

--- a/solution.py
+++ b/solution.py
@@ -9,7 +9,7 @@
 
 LANES = 128
 GROUP = 4
-PIECES = 1
+PIECES = 2
 F32 = jnp.float32
 BF16 = jnp.bfloat16
 

time: 68.2 us -> 68.6 us (level)
  no operation moved by 1% of the time
where the time goes in v4:
time: 68.6 us; the launch traced here: 68.4 us
  Pallas kernels  66.7 us (97%)
  local copies, waits for them, and re-layouts  1.67 us (2%)
    pallas_call x1, Pallas kernels, shards(): pl.pallas_call(functools.partial(kernel, levels, count), out_shape=jax.Sh...  66.7 us
    unnamed x1, local copies, waits for them, and re-layouts  1.67 us

profile of v4, /device:TPU:0, one launch (start us, length us, event | category | flops | bytes accessed | tf_op | source)
XLA Modules:
  0.0 68.4 jit_solution(13804779994703326002)
XLA Ops:
  0.0 66.7 %shard_map.46 = bf16[256,512]{1,0:T(8,128)(2,1)} custom-call(s32[6]{0:T(128)} %bitcast.1, s32[16]{0:T(128)} %owners.1, bf16[1024,512]{1,0:T(8,128)(2,1)} %coef.1, bf16[5,1024,1024]{2,1,0:T(8,128)(2,1)} %transfer.1), custom_call_target="tpu_custom_call" | custom-call | tf_op jit(solution)/shard_map/pallas_call | solution.py:151
  66.7 1.7 %copy.6 = bf16[256,512]{1,0:T(8,128)(2,1)} copy(bf16[256,512]{1,0:T(8,128)(2,1)} %shard_map.46) | data formatting | bytes 524288
